TPU v7x, 1024 devices: a whole 4x8x16 slice. The times are simulated.
1024 devices in a mesh: sub: 128 (over z, y), grp: 8 (over x, core).
Axes of the slice: x: 4, y: 8, z: 16, core: 2. Of those that a mesh axis runs over, the one named last changes fastest.
Arguments:
- rhs: float32 [262144, 512], P(('sub', 'grp')), may hold values from -120 to 120
- kappa: float32 [262144], P(('sub', 'grp')), may hold values from 0.5 to 5
- stiffness: float32 [512, 512], replicated, may hold values from -1 to 3
- local_inverse: float32 [512, 512], replicated, may hold values from -1 to 2
- modes: float32 [8, 512], replicated, may hold values from -0.25 to 0.25
- coarse_weight: float32 [8, 262144], P(None, ('sub', 'grp')), may hold values from 0.5 to 1.5
- coarse_mask: int32 [8, 262144], P(None, ('sub', 'grp')), may hold values 0 or 1
- coarse_inverse: float32 [8192, 8192], P(('sub', 'grp')), may hold values from -1 to 1
- neighbours: int32 [4, 262144], P(None, ('sub', 'grp')), may hold values from -1 to 262143, as said below
Outputs:
- solution: float32 [262144, 512], P(('sub', 'grp'))
Inputs may be any that keep to these rules, and one draw needn't show every extreme that they name: `neighbours`: entries are element numbers or -1. For element e of subdomain d (elements d * 256 to d * 256 + 255), rows 0 and 1 name two other elements of subdomain d, row 2 names an element of subdomain d - 8 or -1, row 3 an element of subdomain d + 8 or -1. Every relation is mutual: row 0 of a names b exactly where row 1 of b names a, and row 3 of a names b exactly where row 2 of b names a. Between subdomains d and d + 8 there are 1 to 64 linked pairs, exactly 64 for some d.
All inputs are finite; a program needn't handle non-finite values. No bound on the sum of `coarse_mask` on one device may be relied on, other than what follows from the above.
Results may differ from a plain program's by a relative error of at most 0.000093.
Values sent between devices are 32-bit elements; how exact they have to be, the bound alone decides.
No kernel may reach another device: no remote copies, remote signals or barrier semaphores. Data moves between devices by JAX's collectives and lax.ppermute only.
A program may use at most 32 MiB of HBM per device.

v0:
```python
import jax
import jax.numpy as jnp
from jax import lax
from jax.sharding import PartitionSpec as P

FACE = 64


SIGMA = 1.0
HIGH = lax.Precision.HIGHEST


def padded(block, sides, width):
    for axis, dim in sides:
        count = lax.axis_size(axis)
        forward = [(i, i + 1) for i in range(count - 1)]
        backward = [(target, source) for source, target in forward]
        low = lax.ppermute(
            lax.slice_in_dim(block, block.shape[dim] - width, None, axis=dim), axis, forward
        )
        high = lax.ppermute(lax.slice_in_dim(block, 0, width, axis=dim), axis, backward)
        block = jnp.concatenate([low, block, high], axis=dim)
    return block


def face_values(field):
    width = field.shape[1]
    return jnp.concatenate([field[:, :FACE], field[:, width - FACE :]], axis=1)


def lift_faces(terms, width):
    middle = jnp.zeros((terms.shape[0], width - 2 * FACE), jnp.float32)
    return jnp.concatenate([terms[:, :FACE], middle, terms[:, FACE:]], axis=1)


def body(
    rhs,
    kappa,
    stiffness,
    local_inverse,
    modes,
    coarse_weight,
    coarse_mask,
    coarse_inverse,
    neighbours,
):
    rows, width = rhs.shape
    groups = lax.axis_size("grp")
    device = lax.axis_index("sub") * groups + lax.axis_index("grp")
    valid = neighbours >= 0
    degree = jnp.sum(valid.astype(jnp.float32), axis=0)
    owner = jnp.floor_divide(neighbours, rows)
    side = jnp.floor_divide(owner - device, groups)
    index = jnp.where(valid, (side + 1) * rows + neighbours - owner * rows, 0)

    def operate(field):
        traces = face_values(field)
        window = padded(traces, (("sub", 0),), rows)
        beside = jnp.sum(jnp.where(valid[:, :, None], window[index], 0.0), axis=0)
        penalty = SIGMA * (degree[:, None] * traces - beside)
        return kappa[:, None] * jnp.dot(field, stiffness, precision=HIGH) + lift_faces(
            penalty, width
        )

    weights = coarse_weight * coarse_mask.astype(jnp.float32)

    def add_coarse(piece):
        return jnp.dot(coarse_inverse, piece, precision=HIGH)

    def precondition(residual):
        local_part = jnp.dot(residual, local_inverse, precision=HIGH) / kappa[:, None]
        projected = jnp.einsum("kp,ep->ke", modes, residual, precision=HIGH)
        restricted = jnp.sum(weights * projected, axis=1)
        solved = add_coarse(lax.all_gather(restricted, ("sub", "grp"), axis=0, tiled=True))
        coarse_part = jnp.dot((weights * solved[:, None]).T, modes, precision=HIGH)
        return local_part + coarse_part

    def dots(values):
        return lax.psum(jnp.stack(values), ("sub", "grp"))

    beta = jnp.sqrt(dots([jnp.sum(rhs * rhs)])[0])
    first = rhs / beta
    z_one = precondition(first)
    w_one = operate(z_one)
    sums = dots([jnp.sum(w_one * first), jnp.sum(w_one * w_one)])
    h11 = sums[0]
    s_one = sums[1]
    h21 = jnp.sqrt(s_one - h11 * h11)
    second = (w_one - h11 * first) / h21
    z_two = precondition(second)
    w_two = operate(z_two)
    sums = dots([jnp.sum(w_two * first), jnp.sum(w_two * second), jnp.sum(w_two * w_two)])
    h12 = sums[0]
    h22 = sums[1]
    s_two = sums[2]
    cross = h11 * h12 + h21 * h22
    det = s_one * s_two - cross * cross
    y_one = beta * (h11 * s_two - h12 * cross) / det
    y_two = beta * (h12 * s_one - h11 * cross) / det
    return y_one * z_one + y_two * z_two


def solution(mesh):
    placed = (
        P(("sub", "grp"), None),
        P(("sub", "grp")),
        P(),
        P(),
        P(),
        P(None, ("sub", "grp")),
        P(None, ("sub", "grp")),
        P(("sub", "grp"), None),
        P(None, ("sub", "grp")),
    )
    return jax.shard_map(
        body, mesh=mesh, in_specs=placed, out_specs=P(("sub", "grp"), None), check_vma=False
    )
```

profile of v0, /device:TPU:1, one launch (start us, length us, event | category | flops | bytes accessed | tf_op | source)
XLA Modules:
  0.0 674.9 jit_solution(768818946201752917)
XLA Ops:
  0.0 1.9 multiply_reduce_fusion.5
  1.9 136.9 %psum.21 = f32[1]{0:T(128)} all-reduce(f32[1]{0:T(128)} %bitcast), channel_id=1, replica_groups=mesh['sub'=128,'grp'=8] {'sub','grp'}, use_global_device_ids=true, to_apply=%region_1.2 | all-reduce | flops 1 | bytes 8 | tf_op jit(solution)/shard_map/psum | solution.py:79
  139.5 0.0 copy-start.5
  139.6 0.7 convert_multiply_fusion
  140.3 0.0 copy-start.4
  140.3 0.6 fusion.6
  140.9 0.3 dynamic-update-slice
  141.2 116.5 %all-reduce = f32[8192]{0:T(1024)S(1)} all-reduce(f32[8192]{0:T(1024)S(1)} %dynamic-update-slice), channel_id=1, replica_groups=mesh['sub'=128,'grp'=8] {'sub','grp'}, use_global_device_ids=true, to_apply=%add | all-reduce | flops 8192 | bytes 65536
  257.7 0.7 convolution_bitcast_fusion.3
  258.4 0.7 fusion.10
  259.1 1.1 fusion
  260.2 0.0 copy-start.2
  260.2 0.1 fusion.25
  260.3 0.1 pad_maximum_fusion.2
  260.4 1.3 collective-permute-start
  261.7 1.3 collective-permute-start.1
  263.0 0.0 copy-start.12
  263.1 0.7 copy-done.12
  263.7 0.6 convert_reduce_fusion
  264.3 0.6 copy-done.9
  264.9 0.7 pad.15.clone
  265.6 0.6 broadcast_clamp_fusion
  266.2 1.8 collective-permute-done.1
  268.0 0.1 pad_maximum_fusion
  268.1 3.3 gather_fusion
  271.5 0.7 copy-done.10
  272.1 0.2 select_reduce_fusion.1
  272.3 0.0 copy-start.21
  272.3 0.6 copy-done.13
  273.0 0.1 multiply_subtract_fusion.1
  273.1 0.1 fusion.27
  273.2 0.0 copy-start.19
  273.2 0.3 copy-done.21
  273.6 0.4 copy-done.16
  274.0 1.8 multiply_reduce_fusion.4
  275.8 1.3 pad_maximum_fusion.4
  277.2 123.3 %psum.22 = f32[2]{0:T(128)S(1)} all-reduce(f32[2]{0:T(128)S(1)} %pad_maximum_fusion.4), channel_id=1, replica_groups=mesh['sub'=128,'grp'=8] {'sub','grp'}, use_global_device_ids=true, to_apply=%region_7.8 | all-reduce | flops 2 | bytes 16 | tf_op jit(solution)/shard_map/psum | solution.py:79
  400.4 0.6 fusion.29
  402.9 0.7 subtract_divide_fusion
  403.6 0.0 copy-done.7
  403.6 0.6 fusion.7
  404.3 0.3 dynamic-update-slice.1
  404.5 117.3 %all-reduce.1 = f32[8192]{0:T(1024)S(1)} all-reduce(f32[8192]{0:T(1024)S(1)} %dynamic-update-slice.1), channel_id=1, replica_groups=mesh['sub'=128,'grp'=8] {'sub','grp'}, use_global_device_ids=true, to_apply=%add.1 | all-reduce | flops 8192 | bytes 65536
  521.9 0.7 convolution_bitcast_fusion.2
  522.5 0.7 fusion.8
  523.3 1.1 fusion.2
  524.3 0.1 fusion.24
  524.4 0.1 pad_maximum_fusion.3
  524.5 1.3 collective-permute-start.2
  525.9 1.3 collective-permute-start.3
  527.2 1.1 collective-permute-done.2
  528.3 3.8 collective-permute-done.3
  532.1 0.1 pad_maximum_fusion.1
  532.2 4.0 gather_fusion.1
  536.2 0.7 copy-done.11
  536.9 1.3 select_reduce_fusion
  538.3 0.1 multiply_subtract_fusion
  538.4 0.1 fusion.26
  538.6 0.7 copy-done.17
  539.2 1.9 multiply_reduce_fusion.2
  541.1 2.0 pad_maximum_fusion.5
  543.1 123.3 %psum.23 = f32[3]{0:T(128)S(1)} all-reduce(f32[3]{0:T(128)S(1)} %pad_maximum_fusion.5), channel_id=1, replica_groups=mesh['sub'=128,'grp'=8] {'sub','grp'}, use_global_device_ids=true, to_apply=%region_13.14 | all-reduce | flops 3 | bytes 24 | tf_op jit(solution)/shard_map/psum | solution.py:79
  666.4 0.7 fusion.28
  674.0 0.9 multiply_add_fusion
  (37 shorter events, 0.1 us)
Async XLA Ops:
  0.0 259.1 %copy-start = (f32[512,512]{1,0:T(8,128)S(1)}, f32[512,512]{1,0:T(8,128)}, u32[]{:S(2)}) copy-start(f32[512,512]{1,0:T(8,128)} %param.12) | copy-start | bytes 3145732
  0.0 140.3 %copy-start.1 = (f32[256,512]{1,0:T(8,128)S(1)}, f32[256,512]{1,0:T(8,128)}, u32[]{:S(2)}) copy-start(f32[256,512]{1,0:T(8,128)} %param.9) | copy-start | bytes 1572868
  1.9 137.6 %copy-start.15 = (f32[8,256]{1,0:T(8,128)S(1)}, f32[8,256]{1,0:T(8,128)}, u32[]{:S(2)}) copy-start(f32[8,256]{1,0:T(8,128)} %param.14) | copy-start | bytes 24580
  139.5 0.7 copy-start.5
  140.3 118.1 %copy-start.6 = (f32[8,256]{1,0:T(8,128)}, f32[8,256]{1,0:T(8,128)S(1)}, u32[]{:S(2)}) copy-start(f32[8,256]{1,0:T(8,128)S(1)} %convert_multiply_fusion) | copy-start | bytes 24580
  140.3 117.4 %copy-start.4 = (f32[8,8192]{1,0:T(8,128)S(1)}, f32[8,8192]{1,0:T(8,128)}, u32[]{:S(2)}) copy-start(f32[8,8192]{1,0:T(8,128)} %param.16) | copy-start | bytes 786436
  258.4 0.7 copy-start.18
  260.2 13.0 %copy-start.2 = (f32[256,512]{1,0:T(8,128)}, f32[256,512]{1,0:T(8,128)S(1)}, u32[]{:S(2)}) copy-start(f32[256,512]{1,0:T(8,128)S(1)} %fusion) | copy-start | bytes 1572868
  260.4 5.7 collective-permute-start
  261.7 6.3 collective-permute-start.1
  263.0 0.7 copy-start.12
  264.3 0.6 copy-start.9
  271.4 0.7 copy-start.10
  272.3 0.6 copy-start.13
  272.3 1.2 copy-start.21
  273.2 0.8 copy-start.16
  273.2 0.8 copy-start.19
  402.9 0.7 copy-start.7
  524.5 7.7 %copy-start.8 = (s32[1024]{0:T(1024)S(1)}, s32[1024]{0:T(1024)}, u32[]{:S(2)}) copy-start(s32[1024]{0:T(1024)} %broadcast_clamp_fusion) | copy-start | bytes 12292
  524.5 3.7 collective-permute-start.2
  525.9 6.3 collective-permute-start.3
  536.2 0.7 copy-start.11
  536.9 1.4 copy-start.14
  536.9 1.6 copy-start.22
  538.5 0.7 copy-start.17
  538.5 0.7 copy-start.20
  539.2 134.8 %copy-start.3 = (f32[256,512]{1,0:T(8,128)S(1)}, f32[256,512]{1,0:T(8,128)}, u32[]{:S(2)}) copy-start(f32[256,512]{1,0:T(8,128)} %copy-done.2) | copy-start | bytes 1572868
where the time goes:
time: 676 us; the launch traced here: 675 us
  blocking collectives  617 us (91%)
  local copies, waits for them, and re-layouts  14.9 us (2%)
  other arithmetic  10.9 us (2%)
  matrix products  9.93 us (1%)
  between operations  9.86 us (1%)
  waiting for transfers between devices  6.82 us (1%)
    psum x3, blocking collectives, dots(): return lax.psum(jnp.stack(values), ('sub', 'grp'))  384 us
    unnamed x2, blocking collectives  234 us
  transfers between devices with their start and end apart: 4, of which 3 were waited for; matrix products, arithmetic and copies ran while one was open for 0% of the time, Pallas kernels for 0%

commit v1 on v0

v1 whole, which is shorter than its diff:
```python
import functools

import jax
import jax.numpy as jnp
from jax import lax
from jax.experimental import pallas as pl
from jax.experimental.pallas import tpu as pltpu
from jax.sharding import PartitionSpec as P

FACE = 64
LANES = 128
KINDS = 8
SIGMA = 1.0
HIGH = lax.Precision.HIGHEST
F32 = jnp.float32
BF16 = jnp.bfloat16


def mm(a, b):
    return jnp.dot(a, b, precision=HIGH, preferred_element_type=F32)


def exact_left(small, value):
    high = value.astype(BF16)
    rest = value - high.astype(F32)
    middle = rest.astype(BF16)
    low = (rest - middle.astype(F32)).astype(BF16)
    width = value.shape[1]
    out = jnp.dot(
        small, jnp.concatenate([high, middle, low], axis=1), preferred_element_type=F32
    )
    return out[:, :width] + (out[:, width : 2 * width] + out[:, 2 * width :])


def total(values):
    return jnp.sum(jnp.sum(values, axis=0, keepdims=True), axis=1, keepdims=True)


def faces(field):
    return jnp.concatenate([field[:, :FACE], field[:, field.shape[1] - FACE :]], axis=1)


def slots(count, groups):
    odd = lax.rem(lax.axis_index("sub"), 2)
    place = lax.axis_index("grp") * KINDS
    return odd * (KINDS * groups) + place, (1 - odd) * (KINDS * groups) + place


def packed_row(values, sums, groups):
    at, sums_at = slots(KINDS, groups)
    lane = lax.broadcasted_iota(jnp.int32, (KINDS, LANES), 1)
    kind = lax.broadcasted_iota(jnp.int32, (KINDS, LANES), 0)
    row = jnp.where(lane == at + kind, jnp.broadcast_to(values, lane.shape), 0.0)
    for n, value in enumerate(sums):
        here = (lane == sums_at + n) & (kind == 0)
        row = jnp.where(here, jnp.broadcast_to(value, lane.shape), row)
    return jnp.sum(row, axis=0, keepdims=True)


def restrict(weights, field, modes):
    return jnp.sum(mm(weights, field) * modes, axis=1, keepdims=True)


def unpack(packed, coarse, count):
    half = packed.shape[0] // 2
    even = packed[pl.ds(0, half, stride=2), :]
    odd = packed[pl.ds(1, half, stride=2), :]
    lane = lax.broadcasted_iota(jnp.int32, (half, LANES), 1)
    low = lane < LANES // 2
    coarse[...] = jnp.where(low, even, odd)
    sums = jnp.sum(jnp.where(low, odd, even), axis=0, keepdims=True)
    kind = lax.rem(lax.broadcasted_iota(jnp.int32, (1, LANES), 1), KINDS)
    return [
        jnp.sum(jnp.where(kind == n, sums, 0.0), axis=1, keepdims=True) for n in range(count)
    ]


def solve_coarse(coarse, own, low, high):
    tiles = coarse.shape[0]
    parts = [[], [], []]
    for group in range(0, tiles, 8):
        partial = [None, None, None]
        for j in range(group, min(group + 8, tiles)):
            vector = jnp.broadcast_to(coarse[pl.ds(j, 1), :], (KINDS, LANES))
            for n, block in enumerate(
                (
                    own[:, j * LANES : (j + 1) * LANES],
                    low[j * KINDS : (j + 1) * KINDS, :],
                    high[j * KINDS : (j + 1) * KINDS, :],
                )
            ):
                term = block * vector
                partial[n] = term if partial[n] is None else partial[n] + term
        for n in range(3):
            parts[n].append(partial[n])
    return [
        jnp.sum(functools.reduce(jnp.add, part), axis=1, keepdims=True) for part in parts
    ]


def at_rows(value, start, rows):
    pieces = [value]
    if start:
        pieces.insert(0, jnp.zeros((start, value.shape[1]), F32))
    rest = rows - start - value.shape[0]
    if rest:
        pieces.append(jnp.zeros((rest, value.shape[1]), F32))
    return jnp.concatenate(pieces, axis=0)


def lifted(field, terms):
    width = field.shape[1]
    head = field[:, :LANES]
    tail = field[:, width - LANES :]
    zeros = jnp.zeros((field.shape[0], FACE), F32)
    head = head + jnp.concatenate([terms[:, :FACE], zeros], axis=1)
    tail = tail + jnp.concatenate([zeros, terms[:, FACE:]], axis=1)
    return jnp.concatenate([head, field[:, LANES : width - LANES], tail], axis=1)


def start_kernel(
    groups,
    rhs,
    kappa,
    local_inverse,
    modes,
    coarse_weight,
    coarse_mask,
    coarse_inverse,
    neighbours,
    row,
    halo,
    local,
    columns,
    links,
    weights,
):
    count = rhs.shape[0]
    subdomain = lax.axis_index("sub") * groups + lax.axis_index("grp")
    base = subdomain * count
    c = coarse_weight[...] * coarse_mask[...].astype(F32)
    weights[...] = c
    field = rhs[...]
    values = restrict(c, field, modes[...])
    row[...] = jnp.broadcast_to(
        packed_row(values, [total(field * field)], groups), row.shape
    )

    named = neighbours[...]
    slot = lax.broadcasted_iota(jnp.int32, named.shape, 0)
    shift = jnp.where(slot == 2, -groups * count, jnp.where(slot == 3, groups * count, 0))
    inside = jnp.where(named >= 0, named - (base + shift), -1).astype(F32)
    stacked = jnp.concatenate(
        [
            inside,
            jnp.broadcast_to(kappa[...], (4, count)),
            c,
            jnp.zeros((LANES - 16, count), F32),
        ],
        axis=0,
    )
    turned = jnp.transpose(stacked)
    columns[...] = turned

    lane = lax.broadcasted_iota(jnp.int32, (count, count), 1)
    line = lax.broadcasted_iota(jnp.int32, (count, count), 0)
    spot = turned[:, :4].astype(jnp.int32)

    def named_by(n):
        return (lane == spot[:, n : n + 1]).astype(F32)

    degree = jnp.sum((turned[:, :4] >= 0.0).astype(F32), axis=1, keepdims=True)
    own = jnp.where(lane == line, degree, 0.0) - (named_by(0) + named_by(1))
    links[:, :count] = (-named_by(2)).astype(BF16)
    links[:, count : 2 * count] = own.astype(BF16)
    links[:, 2 * count :] = (-named_by(3)).astype(BF16)

    solved = mm(field, local_inverse[...]) / turned[:, 4:5]
    local[...] = solved

    tiles = coarse_inverse.shape[1] // LANES
    for j in range(tiles):
        halo[j * KINDS : (j + 1) * KINDS, :] = coarse_inverse[:, j * LANES : (j + 1) * LANES]
    at = tiles * KINDS
    halo[at : at + KINDS, :] = c[:, :LANES]
    halo[at + KINDS : at + 2 * KINDS, :] = c[:, LANES:]
    halo[at + 2 * KINDS :, :] = faces(solved)


def first_kernel(
    groups,
    packed,
    coarse_inverse,
    low,
    high,
    rhs,
    local,
    columns,
    links,
    weights,
    modes,
    stiffness,
    local_inverse,
    row,
    edge,
    z_one,
    w_one,
    next_local,
    beside,
    window,
    scalars,
    coarse,
):
    count = rhs.shape[0]
    square = unpack(packed, coarse, 1)[0]
    beta = jnp.sqrt(square)
    solved = [value / beta for value in solve_coarse(coarse, coarse_inverse, low, high)]
    m = modes[...]
    edges = faces(m)
    turned = columns[...]
    z = local[...] / beta + mm(turned, at_rows(solved[0] * m, 8, LANES))
    z_one[...] = z

    at = (coarse_inverse.shape[1] // LANES) * KINDS

    def weights_of(halo):
        return jnp.concatenate(
            [halo[at : at + KINDS, :], halo[at + KINDS : at + 2 * KINDS, :]], axis=1
        )

    sides = jnp.transpose(at_rows(jnp.concatenate([weights_of(low), weights_of(high)], axis=0), 0, LANES))
    beside[...] = sides
    window[:count, :] = low[at + 2 * KINDS :, :] / beta + mm(
        sides, at_rows(solved[1] * edges, 0, LANES)
    )
    window[count : 2 * count, :] = faces(z)
    window[2 * count :, :] = high[at + 2 * KINDS :, :] / beta + mm(
        sides, at_rows(solved[2] * edges, 8, LANES)
    )
    penalty = SIGMA * exact_left(links[...], window[...])
    kappa = turned[:, 4:5]
    w = lifted(kappa * mm(z, stiffness[...]), penalty)
    w_one[...] = w
    values = restrict(weights[...], w, m)
    sums = [total(w * (rhs[...] / beta)), total(w * w)]
    row[...] = jnp.broadcast_to(packed_row(values, sums, groups), row.shape)
    following = mm(w, local_inverse[...]) / kappa
    next_local[...] = following
    edge[...] = faces(following)
    scalars[...] = jnp.broadcast_to(beta, scalars.shape)


def second_kernel(
    packed,
    coarse_inverse,
    low,
    high,
    low_edge,
    high_edge,
    rhs,
    local,
    columns,
    links,
    modes,
    stiffness,
    beside,
    window,
    z_one,
    w_one,
    scalars,
    row,
    z_two,
    carried,
    coarse,
    frame,
):
    count = rhs.shape[0]
    h11, s_one = unpack(packed, coarse, 2)
    beta = scalars[:1, :1]
    h21 = jnp.sqrt(s_one - h11 * h11)
    solved = solve_coarse(coarse, coarse_inverse, low, high)
    m = modes[...]
    edges = faces(m)
    turned = columns[...]
    sides = beside[...]
    z = local[...] + mm(turned, at_rows(solved[0] * m, 8, LANES))
    z = (z - h11 * z_one[...]) / h21
    z_two[...] = z
    frame[:count, :] = low_edge[...] + mm(sides, at_rows(solved[1] * edges, 0, LANES))
    frame[2 * count :, :] = high_edge[...] + mm(sides, at_rows(solved[2] * edges, 8, LANES))
    frame[:count, :] = (frame[:count, :] - h11 * window[:count, :]) / h21
    frame[2 * count :, :] = (frame[2 * count :, :] - h11 * window[2 * count :, :]) / h21
    frame[count : 2 * count, :] = faces(z)
    penalty = SIGMA * exact_left(links[...], frame[...])
    w = lifted(turned[:, 4:5] * mm(z, stiffness[...]), penalty)
    first = rhs[...] / beta
    second = (w_one[...] - h11 * first) / h21
    lane = lax.broadcasted_iota(jnp.int32, (1, LANES), 1)
    sums = jnp.zeros((1, LANES), F32)
    for n, value in enumerate((total(w * first), total(w * second), total(w * w))):
        sums = jnp.where(lane == n, jnp.broadcast_to(value, sums.shape), sums)
    row[...] = jnp.broadcast_to(sums, row.shape)
    keep = jnp.zeros((1, LANES), F32)
    for n, value in enumerate((beta, h11, s_one, h21)):
        keep = jnp.where(lane == n, jnp.broadcast_to(value, keep.shape), keep)
    carried[...] = jnp.broadcast_to(keep, carried.shape)


def last_kernel(packed, carried, z_one, z_two, out):
    sums = jnp.sum(packed[...], axis=0, keepdims=True)
    h12, h22, s_two = sums[:, 0:1], sums[:, 1:2], sums[:, 2:3]
    kept = carried[:1, :]
    beta, h11, s_one, h21 = (kept[:, n : n + 1] for n in range(4))
    cross = h11 * h12 + h21 * h22
    det = s_one * s_two - cross * cross
    y_one = beta * (h11 * s_two - h12 * cross) / det
    y_two = beta * (h12 * s_one - h11 * cross) / det
    out[...] = y_one * z_one[...] + y_two * z_two[...]


def fan_kernel(rows, out):
    out[...] = jnp.broadcast_to(jnp.sum(rows[...], axis=0, keepdims=True), out.shape)


def body(
    rhs,
    kappa,
    stiffness,
    local_inverse,
    modes,
    coarse_weight,
    coarse_mask,
    coarse_inverse,
    neighbours,
    interpret=False,
):
    count, width = rhs.shape
    groups = lax.axis_size("grp")
    lines = lax.axis_size("sub")
    tall = coarse_inverse.shape[1] // LANES * KINDS + 2 * KINDS + count
    params = pltpu.CompilerParams(vmem_limit_bytes=40 * 1024 * 1024)

    def call(kernel, outs, name, scratch=()):
        return pl.pallas_call(
            kernel,
            out_shape=outs,
            scratch_shapes=list(scratch),
            compiler_params=params,
            name=name,
            interpret=interpret,
        )

    def array(*shape, dtype=F32):
        return jax.ShapeDtypeStruct(shape, dtype)

    def everywhere(row):
        own = lax.all_to_all(row.reshape(groups, 1, LANES), "grp", 0, 0, tiled=True)
        spread = call(fan_kernel, array(lines, LANES), "fan")(own.reshape(groups, LANES))
        every = lax.all_to_all(spread.reshape(lines, 1, LANES), "sub", 0, 0, tiled=True)
        return every.reshape(lines, LANES)

    up = [(i, i + 1) for i in range(lines - 1)]
    down = [(b, a) for a, b in up]

    def exchanged(block):
        return lax.ppermute(block, "sub", up), lax.ppermute(block, "sub", down)

    row, halo, local, columns, links, weights = call(
        functools.partial(start_kernel, groups),
        (
            array(groups, LANES),
            array(tall, LANES),
            array(count, width),
            array(count, LANES),
            array(count, 3 * count, dtype=BF16),
            array(KINDS, count),
        ),
        "start",
    )(
        rhs,
        kappa.reshape(1, count),
        local_inverse,
        modes,
        coarse_weight,
        coarse_mask,
        coarse_inverse,
        neighbours,
    )
    low, high = exchanged(halo)
    packed = everywhere(row)
    row, edge, z_one, w_one, following, beside, window, scalars = call(
        functools.partial(first_kernel, groups),
        (
            array(groups, LANES),
            array(count, LANES),
            array(count, width),
            array(count, width),
            array(count, width),
            array(count, LANES),
            array(3 * count, LANES),
            array(KINDS, LANES),
        ),
        "first",
        [pltpu.VMEM((lines // 2, LANES), F32)],
    )(
        packed,
        coarse_inverse,
        low,
        high,
        rhs,
        local,
        columns,
        links,
        weights,
        modes,
        stiffness,
        local_inverse,
    )
    low_edge, high_edge = exchanged(edge)
    packed = everywhere(row)
    row, z_two, carried = call(
        second_kernel,
        (array(groups, LANES), array(count, width), array(KINDS, LANES)),
        "second",
        [pltpu.VMEM((lines // 2, LANES), F32), pltpu.VMEM((3 * count, LANES), F32)],
    )(
        packed,
        coarse_inverse,
        low,
        high,
        low_edge,
        high_edge,
        rhs,
        following,
        columns,
        links,
        modes,
        stiffness,
        beside,
        window,
        z_one,
        w_one,
        scalars,
    )
    packed = everywhere(row)
    return call(last_kernel, array(count, width), "last")(packed, carried, z_one, z_two)


def solution(mesh, interpret=False):
    placed = (
        P(("sub", "grp"), None),
        P(("sub", "grp")),
        P(),
        P(),
        P(),
        P(None, ("sub", "grp")),
        P(None, ("sub", "grp")),
        P(("sub", "grp"), None),
        P(None, ("sub", "grp")),
    )
    return jax.shard_map(
        functools.partial(body, interpret=interpret),
        mesh=mesh,
        in_specs=placed,
        out_specs=P(("sub", "grp"), None),
        check_vma=False,
    )
```

time: 676 us -> 157 us (0.23)
  blocking collectives: 617 us -> 98.7 us
  starting transfers between devices: 5.18 us -> 18.4 us
  other arithmetic: 10.9 us -> 0 us
  matrix products: 9.93 us -> 0 us
  between operations: 9.86 us -> 0.17 us
  Pallas kernels: 0 us -> 9.28 us
    psum x3 -> x0, blocking collectives: 384 us -> none  [dots(): return lax.psum(jnp.stack(values), ('sub', 'grp'))]
    unnamed x2 -> x0, blocking collectives: 234 us -> none
    all_to_all x0 -> x5, blocking collectives: none -> 98.7 us  [the longest x2 59.4 us: everywhere(): lax.all_to_all(spread.reshape(lines, 1, LANES), 'sub', 0, 0, tiled=True)]
    unnamed x51 -> x64, local copies, waits for them, and re-layouts: 5.26 us -> 21.6 us
    dot_general x10 -> x0, matrix products: 9.93 us -> none  [the longest x2 3.74 us: operate(): jnp.dot(field, stiffness, precision=HIGH)]
    pallas_call x0 -> x7, Pallas kernels: none -> 9.28 us  [the longest x1 3.44 us: body(): call(functools.partial(first_kernel, groups), (array(groups, LANES), arra...]
    gather x2 -> x0, local copies, waits for them, and re-layouts: 7.3 us -> none  [operate(): beside = jnp.sum(jnp.where(valid[:, :, None], window[index], 0.0), axis=0)]
    all_to_all x0 -> x1, starting transfers between devices: none -> 7.17 us  [everywhere(): lax.all_to_all(spread.reshape(lines, 1, LANES), 'sub', 0, 0, tiled=True)]
  transfers between devices with their start and end apart: 4 -> 5, of which waited for: 3 -> 3; matrix products, arithmetic and copies ran while one was open for 0% -> 0% of each run, Pallas kernels for 0% -> 0%
where the time goes in v1:
time: 157 us; the launch traced here: 156 us
  blocking collectives  98.7 us (63%)
  local copies, waits for them, and re-layouts  21.6 us (14%)
  starting transfers between devices  18.4 us (12%)
  Pallas kernels  9.28 us (6%)
  waiting for transfers between devices  8.03 us (5%)
    all_to_all x2, blocking collectives, everywhere(): lax.all_to_all(spread.reshape(lines, 1, LANES), 'sub', 0, 0, tiled=True)  59.4 us
    all_to_all x3, blocking collectives, everywhere(): own = lax.all_to_all(row.reshape(groups, 1, LANES), 'grp', 0, 0, tiled=True)  39.3 us
    unnamed x64, local copies, waits for them, and re-layouts  21.6 us
    ppermute x4, starting transfers between devices, exchanged(): return (lax.ppermute(block, 'sub', up), lax.ppermute(block, 'sub', down))  11.2 us
    all_to_all x1, starting transfers between devices, everywhere(): lax.all_to_all(spread.reshape(lines, 1, LANES), 'sub', 0, 0, tiled=True)  7.17 us
    all_to_all x1, waiting for transfers between devices, everywhere(): lax.all_to_all(spread.reshape(lines, 1, LANES), 'sub', 0, 0, tiled=True)  6.22 us
    pallas_call x1, Pallas kernels, body(): call(functools.partial(first_kernel, groups), (array(groups, LANES), arra...  3.44 us
  transfers between devices with their start and end apart: 5, of which 3 were waited for; matrix products, arithmetic and copies ran while one was open for 0% of the time, Pallas kernels for 0%

profile of v1, /device:TPU:1, one launch (start us, length us, event | category | flops | bytes accessed | tf_op | source)
XLA Modules:
  0.0 156.2 jit_solution(3229531505927960763)
XLA Ops:
  0.0 0.0 copy-start.30
  0.0 0.7 copy-done.30
  0.7 0.0 copy-start
  0.7 1.0 copy-done
  1.7 0.0 copy-start.3
  1.7 1.2 copy-done.3
  2.9 0.0 copy-start.5
  2.9 0.9 copy-done.5
  3.9 0.0 copy-start.16
  3.9 0.7 copy-done.16
  4.6 0.0 copy-start.25
  4.6 0.7 copy-done.25
  5.3 0.0 copy-start.26
  5.3 0.7 copy-done.26
  6.0 0.0 copy-start.27
  6.0 0.7 copy-done.27
  6.7 1.4 start.1
  8.1 0.0 copy-start.11
  8.1 1.3 collective-permute-start.1
  9.4 4.7 %collective-permute-start = (f32[784,128]{1,0:T(8,128)S(1)}, f32[784,128]{1,0:T(8,128)S(1)}, u32[]{:S(2)}, u32[]{:S(2)}) collective-permute-start(f32[784,128]{1,0:T(8,128)S(1)} %get-tuple-element.23), channel_id=1, source_target_pairs={{0,8},{8,16},{16,24},{24,32},{32,40},{40,48},{48,56},{56,64},{64,7... | collective-permute-start | bytes 1204232 | tf_op jit(solution)/shard_map/ppermute | solution.py:366
  14.1 21.0 %all_to_all.30 = f32[8,1,128]{2,1,0:T(1,128)S(1)} all-to-all(f32[8,1,128]{2,1,0:T(1,128)S(1)} %bitcast.34), channel_id=1, replica_groups=mesh['sub'=128,'grp'=8] {'grp'}, dimensions={0} | all-to-all | bytes 8192 | tf_op jit(solution)/shard_map/all_to_all | solution.py:357
  35.1 0.0 copy-start.17
  35.1 31.0 %all_to_all.31 = f32[128,1,128]{2,1,0:T(1,128)S(1)} all-to-all(f32[128,1,128]{2,1,0:T(1,128)S(1)} %bitcast.28), channel_id=1, replica_groups=mesh['sub'=128,'grp'=8] {'sub'}, dimensions={0} | all-to-all | bytes 131072 | tf_op jit(solution)/shard_map/all_to_all | solution.py:359
  66.1 0.0 collective-permute-done.1.high
  66.1 0.0 collective-permute-done.low
  66.1 0.0 copy-done.1
  66.1 0.0 copy-done.2
  66.1 0.0 copy-done.6
  66.1 0.0 copy-done.17
  66.1 0.0 copy-start.4
  66.1 1.2 copy-done.4
  67.3 3.4 %first.1 = (f32[8,128]{1,0:T(8,128)S(1)}, f32[256,128]{1,0:T(8,128)S(1)}, f32[256,512]{1,0:T(8,128)S(1)}, f32[256,512]{1,0:T(8,128)S(1)}, f32[256,512]{1,0:T(8,1...) custom-call(f32[128,128]{1,0:T(8,128)S(1)} %bitcast.25, f32[8,8192]{1,0:T(8,128)S(1)} %copy-done.6, ...), custom_call_target="tpu_custom_call" | custom-call | tf_op jit(solution)/shard_map/first/pallas_call | solution.py:391
  70.8 0.0 copy-done.11
  70.8 0.0 copy-start.7
  70.8 0.8 copy-done.7
  71.6 0.8 copy-done.9
  72.4 0.8 copy-done.13
  73.2 0.7 copy-done.19
  73.8 0.7 copy-done.31
  74.5 9.1 %all_to_all.32 = f32[8,1,128]{2,1,0:T(1,128)S(1)} all-to-all(f32[8,1,128]{2,1,0:T(1,128)S(1)} %bitcast.35), channel_id=1, replica_groups=mesh['sub'=128,'grp'=8] {'grp'}, dimensions={0} | all-to-all | bytes 8192 | tf_op jit(solution)/shard_map/all_to_all | solution.py:357
  83.6 0.0 copy-done.28
  83.6 0.0 copy-start.15
  83.6 0.6 copy-done.15
  84.2 7.2 %all-to-all-start.3 = ((f32[128,1,128]{2,1,0:T(1,128)}), f32[128,1,128]{2,1,0:T(1,128)}, u32[]{:S(2)}, u32[]{:S(2)}) async-start(f32[128,1,128]{2,1,0:T(1,128)} %bitcast.27), calls=%async_computation.3 | async-start | bytes 131072 | tf_op jit(solution)/shard_map/all_to_all | solution.py:359
  91.4 1.3 collective-permute-start.3
  92.7 4.0 %collective-permute-start.2 = (f32[256,128]{1,0:T(8,128)}, f32[256,128]{1,0:T(8,128)S(1)}, u32[]{:S(2)}, u32[]{:S(2)}) collective-permute-start(f32[256,128]{1,0:T(8,128)} %copy-done.31), channel_id=1, source_target_pairs={{0,8},{8,16},{16,24},{24,32},{32,40},{40,48},{48,56},{56,64},{64,7... | collective-permute-start | bytes 393224 | tf_op jit(solution)/shard_map/ppermute | solution.py:366
  96.7 1.7 %collective-permute-done.3.high_edge = f32[256,128]{1,0:T(8,128)S(1)} collective-permute-done((f32[256,128]{1,0:T(8,128)}, f32[256,128]{1,0:T(8,128)S(1)}, u32[]{:S(2)}, u32[]{:S(2)}) %collective-permute-start.3) | collective-permute-done | bytes 131104 | tf_op jit(solution)/shard_map/ppermute | solution.py:366
  98.4 0.6 copy-done.21
  99.1 0.1 collective-permute-done.2.low_edge
  99.2 0.7 copy-done.23
  99.8 6.2 %all-to-all-done.3 = f32[128,1,128]{2,1,0:T(1,128)} async-done(((f32[128,1,128]{2,1,0:T(1,128)}), f32[128,1,128]{2,1,0:T(1,128)}, u32[]{:S(2)}, u32[]{:S(2)}) %all-to-all-start.3) | async-done | bytes 65568 | tf_op jit(solution)/shard_map/all_to_all | solution.py:359
  106.1 0.7 copy-done.29
  106.7 1.0 copy-done.8
  107.8 1.0 copy-done.10
  108.8 0.9 copy-done.12
  109.7 1.0 copy-done.14
  110.7 0.7 copy-done.18
  111.4 0.9 copy-done.20
  112.3 0.9 copy-done.22
  113.3 0.9 copy-done.24
  114.2 3.1 %second.1 = (f32[8,128]{1,0:T(8,128)S(1)}, f32[256,512]{1,0:T(8,128)S(1)}, f32[8,128]{1,0:T(8,128)S(1)}) custom-call(f32[128,128]{1,0:T(8,128)} %bitcast.12.packed, f32[8,8192]{1,0:T(8,128)S(1)} %copy-done.6, f32[784,128]{1,0:T(8,128)S(1)} %collective-permute-done.low, f32[784,128]{1,0:T(8,128)S(1)} %collective-permute-done.1.high, ...), custom_call_target="tpu_custom_call" | custom-call | tf_op jit(solution)/shard_map/second/pallas_call | solution.py:421
  117.3 9.2 %all_to_all.33 = f32[8,1,128]{2,1,0:T(1,128)S(1)} all-to-all(f32[8,1,128]{2,1,0:T(1,128)S(1)} %bitcast.33), channel_id=1, replica_groups=mesh['sub'=128,'grp'=8] {'grp'}, dimensions={0} | all-to-all | bytes 8192 | tf_op jit(solution)/shard_map/all_to_all | solution.py:357
  126.5 28.4 %all_to_all.34 = f32[128,1,128]{2,1,0:T(1,128)S(1)} all-to-all(f32[128,1,128]{2,1,0:T(1,128)S(1)} %bitcast.29), channel_id=1, replica_groups=mesh['sub'=128,'grp'=8] {'sub'}, dimensions={0} | all-to-all | bytes 131072 | tf_op jit(solution)/shard_map/all_to_all | solution.py:359
  154.9 1.3 last.1
  (22 shorter events, 0.1 us)
Async XLA Ops:
  0.0 0.7 copy-start.30
  0.7 1.0 copy-start
  1.7 1.2 copy-start.3
  2.9 0.9 copy-start.5
  3.9 0.7 copy-start.16
  4.6 0.7 copy-start.25
  5.3 0.7 copy-start.26
  6.0 0.7 copy-start.27
  6.7 59.4 %copy-start.1 = (f32[256,512]{1,0:T(8,128)S(1)}, f32[256,512]{1,0:T(8,128)}, u32[]{:S(2)}) copy-start(f32[256,512]{1,0:T(8,128)} %rhs.5) | copy-start | bytes 1572868
  6.7 59.4 %copy-start.2 = (f32[512,512]{1,0:T(8,128)S(1)}, f32[512,512]{1,0:T(8,128)}, u32[]{:S(2)}) copy-start(f32[512,512]{1,0:T(8,128)} %stiffness.3) | copy-start | bytes 3145732
  6.7 59.4 %copy-start.6 = (f32[8,8192]{1,0:T(8,128)S(1)}, f32[8,8192]{1,0:T(8,128)}, u32[]{:S(2)}) copy-start(f32[8,8192]{1,0:T(8,128)} %coarse_inverse.5) | copy-start | bytes 786436
  8.1 62.7 %copy-start.11 = (f32[256,128]{1,0:T(8,128)}, f32[256,128]{1,0:T(8,128)S(1)}, u32[]{:S(2)}) copy-start(f32[256,128]{1,0:T(8,128)S(1)} %get-tuple-element.25.columns) | copy-start | bytes 393220
  8.1 58.0 %collective-permute-start.1 = (f32[784,128]{1,0:T(8,128)S(1)}, f32[784,128]{1,0:T(8,128)S(1)}, u32[]{:S(2)}, u32[]{:S(2)}) collective-permute-start(f32[784,128]{1,0:T(8,128)S(1)} %get-tuple-element.23), channel_id=1, source_target_pairs={{8,0},{16,8},{24,16},{32,24},{40,32},{48,40},{56,48},{64,56},{72,6... | collective-permute-start | bytes 1204232 | tf_op jit(solution)/shard_map/ppermute | solution.py:366
  9.4 56.7 %collective-permute-start = (f32[784,128]{1,0:T(8,128)S(1)}, f32[784,128]{1,0:T(8,128)S(1)}, u32[]{:S(2)}, u32[]{:S(2)}) collective-permute-start(f32[784,128]{1,0:T(8,128)S(1)} %get-tuple-element.23), channel_id=1, source_target_pairs={{0,8},{8,16},{16,24},{24,32},{32,40},{40,48},{48,56},{56,64},{64,7... | collective-permute-start | bytes 1204232 | tf_op jit(solution)/shard_map/ppermute | solution.py:366
  35.1 31.0 %copy-start.17 = (f32[8,512]{1,0:T(8,128)S(1)}, f32[8,512]{1,0:T(8,128)}, u32[]{:S(2)}) copy-start(f32[8,512]{1,0:T(8,128)} %modes.5) | copy-start | bytes 49156
  66.1 1.2 copy-start.4
  70.8 0.8 copy-start.7
  71.6 0.8 copy-start.9
  72.4 0.8 copy-start.13
  73.2 0.7 copy-start.19
  73.8 0.7 copy-start.31
  74.5 9.1 %copy-start.28 = (f32[8,128]{1,0:T(8,128)}, f32[8,128]{1,0:T(8,128)S(1)}, u32[]{:S(2)}) copy-start(f32[8,128]{1,0:T(8,128)S(1)} %get-tuple-element.35.scalars) | copy-start | bytes 12292
  83.6 0.6 copy-start.15
  84.2 21.8 %all-to-all-start.3 = ((f32[128,1,128]{2,1,0:T(1,128)}), f32[128,1,128]{2,1,0:T(1,128)}, u32[]{:S(2)}, u32[]{:S(2)}) async-start(f32[128,1,128]{2,1,0:T(1,128)} %bitcast.27), calls=%async_computation.3 | async-start | bytes 131072 | tf_op jit(solution)/shard_map/all_to_all | solution.py:359
  91.4 7.0 %collective-permute-start.3 = (f32[256,128]{1,0:T(8,128)}, f32[256,128]{1,0:T(8,128)S(1)}, u32[]{:S(2)}, u32[]{:S(2)}) collective-permute-start(f32[256,128]{1,0:T(8,128)} %copy-done.31), channel_id=1, source_target_pairs={{8,0},{16,8},{24,16},{32,24},{40,32},{48,40},{56,48},{64,56},{72,6... | collective-permute-start | bytes 393224 | tf_op jit(solution)/shard_map/ppermute | solution.py:366
  92.7 6.5 %collective-permute-start.2 = (f32[256,128]{1,0:T(8,128)}, f32[256,128]{1,0:T(8,128)S(1)}, u32[]{:S(2)}, u32[]{:S(2)}) collective-permute-start(f32[256,128]{1,0:T(8,128)} %copy-done.31), channel_id=1, source_target_pairs={{0,8},{8,16},{16,24},{24,32},{32,40},{40,48},{48,56},{56,64},{64,7... | collective-permute-start | bytes 393224 | tf_op jit(solution)/shard_map/ppermute | solution.py:366
  98.4 0.6 copy-start.21
  99.2 0.7 copy-start.23
  106.1 0.7 copy-start.29
  106.7 1.0 copy-start.8
  107.8 1.0 copy-start.10
  108.8 0.9 copy-start.12
  109.7 1.0 copy-start.14
  110.7 0.7 copy-start.18
  111.4 0.9 copy-start.20
  112.3 0.9 copy-start.22
  113.3 0.9 copy-start.24
